TPU v7x, 32 devices: a whole 2x2x4 slice. The times are simulated.
32 devices in a mesh: row: 8 (over y, x, core), col: 4 (over z).
Axes of the slice: x: 2, y: 2, z: 4, core: 2. Of those that a mesh axis runs over, the one named last changes fastest.
Arguments:
- matrix: float32 [8, 3, 256, 4, 6, 256], P('row', None, None, 'col'), as said below
- checksum: float32 [8, 3, 256, 6, 256], P('row'), as said below
- failed: int32 [4], P('col'), may hold values from 0 to 3, as said below
Outputs:
- factored: float32 [8, 3, 256, 4, 6, 256], P('row', None, None, 'col')
- updated_checksum_result: float32 [8, 3, 256, 6, 256], P('row')
Inputs may be any that keep to these rules, and one draw needn't show every extreme that they name: `failed`: a permutation of the grid column indices; entry 0 names the grid column whose tiles in matrix carry no information. With the lost grid column rebuilt from checksum, matrix is symmetric positive definite. `checksum`: for each grid row, the sum over all grid columns of the intact matrix's tiles, the lost column included.
All inputs are finite; a program needn't handle non-finite values.
Results may differ from a plain program's by a relative error of at most 0.0003.
Values sent between devices are 32-bit elements; how exact they have to be, the bound alone decides.
A program may use at most 128 MiB of HBM per device.

v0:
```python
import jax
import jax.numpy as jnp
from jax import lax
from jax.sharding import PartitionSpec as P

PANELS = 3


def spread_2(block, axis, holder):
    block = jnp.where(lax.axis_index(axis) == holder, block, jnp.zeros_like(block))
    return lax.psum(block, axis)


def solve_panel(column, factor, row_tiles, panel):
    tile_count, width = (column.shape[0], column.shape[1])
    stacked = column.reshape(tile_count * width, width)
    solved = jax.scipy.linalg.solve_triangular(factor, stacked.T, lower=True).T.reshape(
        tile_count, width, width
    )
    chosen = jnp.where((row_tiles > panel)[:, None, None], solved, 0.0)
    return jnp.where((row_tiles == panel)[:, None, None], factor[None, :, :], chosen)


def matching_tiles(panel_rows, column_position, rows_count, cols_count):
    width = panel_rows.shape[1]
    repeats = max(rows_count // cols_count, 1)
    received = []
    for offset in range(repeats):
        source = (column_position + offset * cols_count) % rows_count
        received.append(spread_2(panel_rows, "row", source))
    return jnp.stack(received, axis=1).reshape(-1, width, width)


def shards(matrix, checksum, failed):
    rows_count = lax.axis_size("row")
    cols_count = lax.axis_size("col")
    row_index = lax.axis_index("row")
    column_position = lax.axis_index("col")
    tile_rows, width, tile_cols = (matrix.shape[1], matrix.shape[2], matrix.shape[4])
    resident_tiles = matrix.reshape(tile_rows, width, tile_cols, width)
    totals = checksum.reshape(tile_rows, width, tile_cols, width)
    missing_tiles = lax.all_gather(failed, "col", axis=0, tiled=True)[0]
    healthy_member = jnp.where(column_position != missing_tiles, resident_tiles, 0.0)
    remaining_peers = lax.psum(healthy_member, "col")
    work = jnp.where(column_position == missing_tiles, totals - remaining_peers, resident_tiles)
    row_tiles = row_index + jnp.arange(tile_rows, dtype=jnp.int32) * rows_count
    col_tiles = column_position + jnp.arange(tile_cols, dtype=jnp.int32) * cols_count
    identity = jnp.eye(width, dtype=jnp.float32)
    finished = []
    for panel in range(PANELS):
        col_root = panel % cols_count
        col_slot = panel // cols_count
        row_root = panel % rows_count
        row_slot = panel // rows_count
        column = work[:, :, col_slot, :]
        owner = jnp.logical_and(row_index == row_root, column_position == col_root)
        diag_input = jnp.where(owner, work[row_slot, :, col_slot, :], identity)
        factor_here = jnp.linalg.cholesky(diag_input)
        factor = spread_2(factor_here, "row", row_root)
        own_rows = solve_panel(column, factor, row_tiles, panel)
        panel_rows = spread_2(own_rows, "col", col_root)
        panel_cols = matching_tiles(panel_rows, column_position, rows_count, cols_count)
        update = jnp.einsum(
            "axr,byr->axby", panel_rows, panel_cols, precision=lax.Precision.HIGHEST
        )
        work = work - update
        finished.append((col_root, col_slot, panel_rows))
    totals = lax.psum(work, "col")
    for col_root, col_slot, panel_rows in finished:
        current = work[:, :, col_slot, :]
        work = work.at[:, :, col_slot, :].set(
            jnp.where(column_position == col_root, panel_rows, current)
        )
    keep = (row_tiles[:, None] >= col_tiles[None, :])[:, None, :, None]
    factored = jnp.where(keep, work, 0.0).reshape(matrix.shape)
    return (factored, totals.reshape(checksum.shape))


def solution(mesh):
    return jax.shard_map(
        shards,
        mesh=mesh,
        in_specs=(
            P("row", None, None, "col", None, None),
            P("row", None, None, None, None),
            P("col"),
        ),
        out_specs=(P("row", None, None, "col", None, None), P("row", None, None, None, None)),
        check_vma=False,
    )
```

profile of v0, /device:TPU:0, one launch (start us, length us, event | category | flops | bytes accessed | tf_op | source)
XLA Modules:
  0.0 1121.8 jit_solution(12888516157622875369)
XLA Ops:
  9.9 9.9 all-reduce.1
  19.8 12.1 %copy.25 = f32[1,3,256,1,6,256]{2,5,4,1,3,0:T(8,128)} copy(f32[1,3,256,1,6,256]{5,3,4,2,1,0:T(1,128)} %param.12) | data formatting | bytes 9437184 | tf_op args[0]
  43.1 165.1 %all-reduce.17.cloned.1.call-done = f32[3,256,6,256]{1,3,2,0:T(8,128)} async-done(((f32[3,256,6,256]{1,3,2,0:T(8,128)}), f32[3,256,6,256]{1,3,2,0:T(8,128)}) %all-reduce.17.cloned.1.call-update) | async-done | bytes 4718608 | tf_op jit(solution)/shard_map/psum | solution.py:44
  217.9 11.7 %cholesky.172 = f32[128,128]{1,0:T(8,128)S(1)} custom-call(f32[128,128]{1,0:T(8,128)S(1)} %cholesky.270), custom_call_target="Cholesky" | custom-call | tf_op jit(solution)/shard_map/jit(cholesky)/cholesky | solution.py:58
  229.7 9.8 custom-call.15
  240.0 11.7 %cholesky.189 = f32[128,128]{1,0:T(8,128)S(1)} custom-call(f32[128,128]{1,0:T(8,128)S(1)} %convolution_subtract_fusion.8), custom_call_target="Cholesky" | custom-call | tf_op jit(solution)/shard_map/jit(cholesky)/cholesky | solution.py:58
  255.1 52.3 %all-reduce.19.cloned.1.call-done = f32[256,256]{1,0:T(8,128)} async-done(((f32[256,256]{1,0:T(8,128)}), f32[256,256]{1,0:T(8,128)}) %all-reduce.19.cloned.1.call-update) | async-done | bytes 262160 | tf_op jit(solution)/shard_map/psum | solution.py:11
  312.5 19.7 %custom-call.16 = f32[2,128,128]{1,2,0:T(8,128)S(1)} custom-call(f32[2,128,128]{2,1,0:T(8,128)S(1)} %get-tuple-element.60), custom_call_target="InvertDiagBlocksLowerTriangular" | custom-call | tf_op jit(solution)/shard_map/jit(_solve_triangular)/triangular_solve | solution.py:17
  335.9 43.3 %all-reduce.21.cloned.1.call-done = f32[3,256,256]{1,2,0:T(8,128)} async-done(((f32[3,256,256]{1,2,0:T(8,128)}), f32[3,256,256]{1,2,0:T(8,128)}) %all-reduce.21.cloned.1.call-update) | async-done | bytes 786448 | tf_op jit(solution)/shard_map/psum | solution.py:11
  381.8 59.4 %all-reduce.37.cloned.1.call-done = (f32[3,1,256,256]{2,3,0,1:T(8,128)}, f32[3,1,256,256]{2,3,0,1:T(8,128)}) async-done(((f32[3,1,256,256]{2,3,0,1:T(8,128)}, f32[3,1,256,256]{2,3,0,1:T(8,128)}), (f32[3,1,256,256]{2,3,0,1:T(8,128)}, f32[3,1,256,256]{2,3,0,1:T(8,128)})) %all-reduce.37.cloned.1.call-update) | async-done | bytes 1572880 | tf_op jit(solution)/shard_map/psum | solution.py:11
  455.1 11.7 %cholesky.206 = f32[128,128]{1,0:T(8,128)S(1)} custom-call(f32[128,128]{1,0:T(8,128)S(1)} %cholesky.273), custom_call_target="Cholesky" | custom-call | tf_op jit(solution)/shard_map/jit(cholesky)/cholesky | solution.py:58
  477.8 11.9 %cholesky.223 = f32[128,128]{1,0:T(8,128)S(1)} custom-call(f32[128,128]{1,0:T(8,128)S(1)} %convolution_subtract_fusion.7), custom_call_target="Cholesky" | custom-call | tf_op jit(solution)/shard_map/jit(cholesky)/cholesky | solution.py:58
  492.7 52.9 %all-reduce.23.cloned.1.call-done = f32[256,256]{1,0:T(8,128)} async-done(((f32[256,256]{1,0:T(8,128)}), f32[256,256]{1,0:T(8,128)}) %all-reduce.23.cloned.1.call-update) | async-done | bytes 262160 | tf_op jit(solution)/shard_map/psum | solution.py:11
  550.6 19.7 %custom-call.18 = f32[2,128,128]{1,2,0:T(8,128)S(1)} custom-call(f32[2,128,128]{2,1,0:T(8,128)S(1)} %get-tuple-element.61), custom_call_target="InvertDiagBlocksLowerTriangular" | custom-call | tf_op jit(solution)/shard_map/jit(_solve_triangular)/triangular_solve | solution.py:17
  574.0 43.4 %all-reduce.25.cloned.1.call-done = f32[3,256,256]{1,2,0:T(8,128)} async-done(((f32[3,256,256]{1,2,0:T(8,128)}), f32[3,256,256]{1,2,0:T(8,128)}) %all-reduce.25.cloned.1.call-update) | async-done | bytes 786448 | tf_op jit(solution)/shard_map/psum | solution.py:11
  620.2 59.3 %all-reduce.35.cloned.1.call-done = (f32[3,1,256,256]{2,3,0,1:T(8,128)}, f32[3,1,256,256]{2,3,0,1:T(8,128)}) async-done(((f32[3,1,256,256]{2,3,0,1:T(8,128)}, f32[3,1,256,256]{2,3,0,1:T(8,128)}), (f32[3,1,256,256]{2,3,0,1:T(8,128)}, f32[3,1,256,256]{2,3,0,1:T(8,128)})) %all-reduce.35.cloned.1.call-update) | async-done | bytes 1572880 | tf_op jit(solution)/shard_map/psum | solution.py:11
  696.0 11.7 %cholesky.240 = f32[128,128]{1,0:T(8,128)S(1)} custom-call(f32[128,128]{1,0:T(8,128)S(1)} %cholesky.276), custom_call_target="Cholesky" | custom-call | tf_op jit(solution)/shard_map/jit(cholesky)/cholesky | solution.py:58
  718.7 11.9 %cholesky.257 = f32[128,128]{1,0:T(8,128)S(1)} custom-call(f32[128,128]{1,0:T(8,128)S(1)} %convolution_subtract_fusion.6), custom_call_target="Cholesky" | custom-call | tf_op jit(solution)/shard_map/jit(cholesky)/cholesky | solution.py:58
  733.7 52.9 %all-reduce.27.cloned.1.call-done = f32[256,256]{1,0:T(8,128)} async-done(((f32[256,256]{1,0:T(8,128)}), f32[256,256]{1,0:T(8,128)}) %all-reduce.27.cloned.1.call-update) | async-done | bytes 262160 | tf_op jit(solution)/shard_map/psum | solution.py:11
  791.6 19.7 %custom-call.20 = f32[2,128,128]{1,2,0:T(8,128)S(1)} custom-call(f32[2,128,128]{2,1,0:T(8,128)S(1)} %get-tuple-element.62), custom_call_target="InvertDiagBlocksLowerTriangular" | custom-call | tf_op jit(solution)/shard_map/jit(_solve_triangular)/triangular_solve | solution.py:17
  815.0 43.4 %all-reduce.29.cloned.1.call-done = f32[3,256,256]{1,2,0:T(8,128)} async-done(((f32[3,256,256]{1,2,0:T(8,128)}), f32[3,256,256]{1,2,0:T(8,128)}) %all-reduce.29.cloned.1.call-update) | async-done | bytes 786448 | tf_op jit(solution)/shard_map/psum | solution.py:11
  861.3 59.1 %all-reduce.33.cloned.1.call-done = (f32[3,1,256,256]{2,3,0,1:T(8,128)}, f32[3,1,256,256]{2,3,0,1:T(8,128)}) async-done(((f32[3,1,256,256]{2,3,0,1:T(8,128)}, f32[3,1,256,256]{2,3,0,1:T(8,128)}), (f32[3,1,256,256]{2,3,0,1:T(8,128)}, f32[3,1,256,256]{2,3,0,1:T(8,128)})) %all-reduce.33.cloned.1.call-update) | async-done | bytes 1572880 | tf_op jit(solution)/shard_map/psum | solution.py:11
  947.4 12.1 %copy.53 = f32[1,3,256,1,6,256]{5,3,4,2,1,0:T(1,128)} copy(f32[1,3,256,1,6,256]{2,5,4,1,3,0:T(8,128)} %select_bitcast_fusion) | data formatting | bytes 9437184
  959.5 149.2 %all-reduce.31.cloned.1.call-done = f32[1,3,256,6,256]{2,4,3,1,0:T(8,128)} async-done(((f32[1,3,256,6,256]{2,4,3,1,0:T(8,128)}), f32[1,3,256,6,256]{2,4,3,1,0:T(8,128)}) %all-reduce.31.cloned.1.call-update) | async-done | bytes 4718608 | tf_op jit(solution)/shard_map/psum | solution.py:68
  (172 shorter events, 160.2 us)
Async XLA Ops:
  7.2 201.1 %all-reduce.17.cloned.1.call-start = ((), (), s32[]{:S(2)}) async-start(), calls=%async_computation | async-start | bytes 9437184 | tf_op jit(solution)/shard_map/psum | solution.py:44
  36.9 270.5 %all-reduce.19.cloned.1.call-start = ((), (), s32[]{:S(2)}) async-start(), calls=%async_computation.1 | async-start | bytes 524288 | tf_op jit(solution)/shard_map/psum | solution.py:11
  214.5 2.2 copy-start.1
  216.7 38.1 %slice-start = ((f32[3,256,6,256]{1,3,2,0:T(8,128)}), f32[3,256,1,256]{1,3,2,0:T(8,128)S(1)}, s32[]{:S(2)}) async-start(f32[3,256,6,256]{1,3,2,0:T(8,128)} %copy-done.1), calls=%async_computation.11 | async-start | bytes 1572864 | tf_op jit(solution)/shard_map/slice | solution.py:55
  254.4 124.9 %all-reduce.21.cloned.1.call-start = ((), (), s32[]{:S(2)}) async-start(), calls=%async_computation.2 | async-start | bytes 1572864 | tf_op jit(solution)/shard_map/psum | solution.py:11
  307.4 27.3 %copy-start.7 = (f32[256,256]{1,0:T(8,128)S(1)}, f32[256,256]{1,0:T(8,128)}, u32[]{:S(2)}) copy-start(f32[256,256]{1,0:T(8,128)} %all-reduce.19.cloned.1.call-done) | copy-start | bytes 786436
  335.8 105.4 %all-reduce.37.cloned.1.call-start = ((), (), s32[]{:S(2)}) async-start(), calls=%async_computation.10 | async-start | bytes 3145728 | tf_op jit(solution)/shard_map/psum | solution.py:11
  379.3 65.0 %copy-start.5 = (f32[3,256,256]{1,2,0:T(8,128)S(1)}, f32[3,256,256]{1,2,0:T(8,128)}, u32[]{:S(2)}) copy-start(f32[3,256,256]{1,2,0:T(8,128)} %all-reduce.21.cloned.1.call-done) | copy-start | bytes 2359300
  381.8 163.8 %all-reduce.23.cloned.1.call-start = ((), (), s32[]{:S(2)}) async-start(), calls=%async_computation.3 | async-start | bytes 524288 | tf_op jit(solution)/shard_map/psum | solution.py:11
  451.7 2.2 copy-start.2
  453.9 38.5 %slice-start.1 = ((f32[3,256,6,256]{1,3,2,0:T(8,128)}), f32[3,256,1,256]{1,3,2,0:T(8,128)S(1)}, s32[]{:S(2)}) async-start(f32[3,256,6,256]{1,3,2,0:T(8,128)} %copy-done.2), calls=%async_computation.12 | async-start | bytes 1572864 | tf_op jit(solution)/shard_map/slice | solution.py:55
  492.3 125.1 %all-reduce.25.cloned.1.call-start = ((), (), s32[]{:S(2)}) async-start(), calls=%async_computation.4 | async-start | bytes 1572864 | tf_op jit(solution)/shard_map/psum | solution.py:11
  545.6 27.2 %copy-start.9 = (f32[256,256]{1,0:T(8,128)S(1)}, f32[256,256]{1,0:T(8,128)}, u32[]{:S(2)}) copy-start(f32[256,256]{1,0:T(8,128)} %all-reduce.23.cloned.1.call-done) | copy-start | bytes 786436
  574.0 105.5 %all-reduce.35.cloned.1.call-start = ((), (), s32[]{:S(2)}) async-start(), calls=%async_computation.9 | async-start | bytes 3145728 | tf_op jit(solution)/shard_map/psum | solution.py:11
  617.4 67.8 %copy-start.4 = (f32[3,256,256]{1,2,0:T(8,128)S(1)}, f32[3,256,256]{1,2,0:T(8,128)}, u32[]{:S(2)}) copy-start(f32[3,256,256]{1,2,0:T(8,128)} %all-reduce.25.cloned.1.call-done) | copy-start | bytes 2359300
  619.9 166.7 %all-reduce.27.cloned.1.call-start = ((), (), s32[]{:S(2)}) async-start(), calls=%async_computation.5 | async-start | bytes 524288 | tf_op jit(solution)/shard_map/psum | solution.py:11
  692.6 2.2 copy-start.3
  694.8 38.6 %slice-start.2 = ((f32[3,256,6,256]{1,3,2,0:T(8,128)}), f32[3,256,1,256]{1,3,2,0:T(8,128)S(1)}, s32[]{:S(2)}) async-start(f32[3,256,6,256]{1,3,2,0:T(8,128)} %copy-done.3), calls=%async_computation.13 | async-start | bytes 1572864 | tf_op jit(solution)/shard_map/slice | solution.py:55
  733.3 125.1 %all-reduce.29.cloned.1.call-start = ((), (), s32[]{:S(2)}) async-start(), calls=%async_computation.6 | async-start | bytes 1572864 | tf_op jit(solution)/shard_map/psum | solution.py:11
  786.6 27.2 %copy-start.8 = (f32[256,256]{1,0:T(8,128)S(1)}, f32[256,256]{1,0:T(8,128)}, u32[]{:S(2)}) copy-start(f32[256,256]{1,0:T(8,128)} %all-reduce.27.cloned.1.call-done) | copy-start | bytes 786436
  815.0 105.4 %all-reduce.33.cloned.1.call-start = ((), (), s32[]{:S(2)}) async-start(), calls=%async_computation.8 | async-start | bytes 3145728 | tf_op jit(solution)/shard_map/psum | solution.py:11
  858.4 67.7 %copy-start.6 = (f32[3,256,256]{1,2,0:T(8,128)S(1)}, f32[3,256,256]{1,2,0:T(8,128)}, u32[]{:S(2)}) copy-start(f32[3,256,256]{1,2,0:T(8,128)} %all-reduce.29.cloned.1.call-done) | copy-start | bytes 2359300
  860.9 247.8 %all-reduce.31.cloned.1.call-start = ((), (), s32[]{:S(2)}) async-start(), calls=%async_computation.7 | async-start | bytes 9437184 | tf_op jit(solution)/shard_map/psum | solution.py:68
  933.1 2.2 copy-start
Sparse Core Ops, SparseCore 0:
  37.0 171.1 all-reduce.16
  254.5 52.8 all-reduce.18
  336.0 43.2 all-reduce.20
  383.0 58.2 all-reduce.36
  492.4 53.0 all-reduce.22
  574.1 43.2 all-reduce.24
  621.2 58.2 all-reduce.34
  733.4 53.0 all-reduce.26
  815.1 43.2 all-reduce.28
  862.1 58.2 all-reduce.32
  937.6 171.1 all-reduce.30
where the time goes:
time: 1130 us; the launch traced here: 1120 us
  waiting for transfers between devices  780 us (69%)
  other arithmetic  209 us (18%)
  local copies, waits for them, and re-layouts  72.9 us (6%)
  matrix products  28.6 us (3%)
  between operations  19.4 us (2%)
    psum x9, waiting for transfers between devices, spread_2(): return lax.psum(block, axis)  466 us
    psum x1, waiting for transfers between devices, shards(): remaining_peers = lax.psum(healthy_member, 'col')  165 us
    psum x1, waiting for transfers between devices, shards(): totals = lax.psum(work, 'col')  149 us
    another operation x20, other arithmetic, shards(): factor_here = jnp.linalg.cholesky(diag_input)  103 us
    another operation x7, other arithmetic, solve_panel(): jax.scipy.linalg.solve_triangular(factor, stacked.T, lower=True)  62.1 us
    unnamed x28, local copies, waits for them, and re-layouts  49.2 us
  transfers between devices with their start and end apart: 11, of which 11 were waited for; matrix products, arithmetic and copies ran while one was open for 3% of the time, Pallas kernels for 0%

commit v1 on v0

--- a/solution.py
+++ b/solution.py
@@ -41,7 +41,11 @@
     totals = checksum.reshape(tile_rows, width, tile_cols, width)
     missing_tiles = lax.all_gather(failed, "col", axis=0, tiled=True)[0]
     healthy_member = jnp.where(column_position != missing_tiles, resident_tiles, 0.0)
-    remaining_peers = lax.psum(healthy_member, "col")
+    remaining_peers = healthy_member
+    for hop in (1, 2):
+        remaining_peers = remaining_peers + lax.ppermute(
+            remaining_peers, "col", [(dev, dev ^ hop) for dev in range(4)]
+        )
     work = jnp.where(column_position == missing_tiles, totals - remaining_peers, resident_tiles)
     row_tiles = row_index + jnp.arange(tile_rows, dtype=jnp.int32) * rows_count
     col_tiles = column_position + jnp.arange(tile_cols, dtype=jnp.int32) * cols_count

time: 1130 us -> 1270 us (1.12)
  waiting for transfers between devices: 780 us -> 912 us
    ppermute x0 -> x2, waiting for transfers between devices: none -> 297 us  [shards(): lax.ppermute(remaining_peers, 'col', [(dev, dev ^ hop) for dev in range(4)])]
    psum x1 -> x0, waiting for transfers between devices: 165 us -> none  [shards(): remaining_peers = lax.psum(healthy_member, 'col')]
    unnamed x28 -> x30, local copies, waits for them, and re-layouts: 49.2 us -> 49.2 us
  transfers between devices with their start and end apart: 11 -> 12, of which waited for: 11 -> 12; matrix products, arithmetic and copies ran while one was open for 3% -> 2% of each run, Pallas kernels for 0% -> 0%
where the time goes in v1:
time: 1270 us; the launch traced here: 1260 us
  waiting for transfers between devices  912 us (72%)
  other arithmetic  211 us (17%)
  local copies, waits for them, and re-layouts  73.2 us (6%)
  matrix products  28.6 us (2%)
  between operations  20.1 us (2%)
    psum x9, waiting for transfers between devices, spread_2(): return lax.psum(block, axis)  466 us
    ppermute x2, waiting for transfers between devices, shards(): lax.ppermute(remaining_peers, 'col', [(dev, dev ^ hop) for dev in range(4)])  297 us
    psum x1, waiting for transfers between devices, shards(): totals = lax.psum(work, 'col')  149 us
    another operation x20, other arithmetic, shards(): factor_here = jnp.linalg.cholesky(diag_input)  104 us
    another operation x7, other arithmetic, solve_panel(): jax.scipy.linalg.solve_triangular(factor, stacked.T, lower=True)  62.1 us
    unnamed x30, local copies, waits for them, and re-layouts  49.2 us
  transfers between devices with their start and end apart: 12, of which 12 were waited for; matrix products, arithmetic and copies ran while one was open for 2% of the time, Pallas kernels for 0%

profile of v1, /device:TPU:0, one launch (start us, length us, event | category | flops | bytes accessed | tf_op | source)
XLA Modules:
  0.0 1258.5 jit_solution(13722917386310519270)
XLA Ops:
  9.9 9.9 all-reduce.1
  19.8 12.1 copy.25
  36.5 99.9 %collective-permute-done = f32[3,256,6,256]{1,3,2,0:T(8,128)S(1)} collective-permute-done((f32[3,256,6,256]{1,3,2,0:T(8,128)S(1)}, f32[3,256,6,256]{1,3,2,0:T(8,128)S(1)}, u32[]{:S(2)}, u32[]{:S(2)}) %collective-permute-start) | collective-permute-done | bytes 4718624 | tf_op jit(solution)/shard_map/ppermute | solution.py:46
  145.5 196.7 %collective-permute-done.1 = f32[3,256,6,256]{1,3,2,0:T(8,128)} collective-permute-done((f32[3,256,6,256]{1,3,2,0:T(8,128)}, f32[3,256,6,256]{1,3,2,0:T(8,128)}, u32[]{:S(2)}, u32[]{:S(2)}) %collective-permute-start.1) | collective-permute-done | bytes 4718624 | tf_op jit(solution)/shard_map/ppermute | solution.py:46
  353.4 11.7 cholesky.172
  375.5 11.7 cholesky.189
  390.7 52.2 %all-reduce.16.cloned.1.call-done = f32[256,256]{1,0:T(8,128)} async-done(((f32[256,256]{1,0:T(8,128)}), f32[256,256]{1,0:T(8,128)}) %all-reduce.16.cloned.1.call-update) | async-done | bytes 262160 | tf_op jit(solution)/shard_map/psum | solution.py:11
  448.2 19.7 %custom-call.16 = f32[2,128,128]{1,2,0:T(8,128)S(1)} custom-call(f32[2,128,128]{2,1,0:T(8,128)S(1)} %get-tuple-element.60), custom_call_target="InvertDiagBlocksLowerTriangular" | custom-call | tf_op jit(solution)/shard_map/jit(_solve_triangular)/triangular_solve | solution.py:17
  471.6 43.3 %all-reduce.18.cloned.1.call-done = f32[3,256,256]{1,2,0:T(8,128)} async-done(((f32[3,256,256]{1,2,0:T(8,128)}), f32[3,256,256]{1,2,0:T(8,128)}) %all-reduce.18.cloned.1.call-update) | async-done | bytes 786448 | tf_op jit(solution)/shard_map/psum | solution.py:11
  517.6 59.5 %all-reduce.34.cloned.1.call-done = (f32[3,1,256,256]{2,3,0,1:T(8,128)}, f32[3,1,256,256]{2,3,0,1:T(8,128)}) async-done(((f32[3,1,256,256]{2,3,0,1:T(8,128)}, f32[3,1,256,256]{2,3,0,1:T(8,128)}), (f32[3,1,256,256]{2,3,0,1:T(8,128)}, f32[3,1,256,256]{2,3,0,1:T(8,128)})) %all-reduce.34.cloned.1.call-update) | async-done | bytes 1572880 | tf_op jit(solution)/shard_map/psum | solution.py:11
  591.0 11.7 cholesky.206
  613.1 11.9 cholesky.223
  628.8 52.9 %all-reduce.20.cloned.1.call-done = f32[256,256]{1,0:T(8,128)} async-done(((f32[256,256]{1,0:T(8,128)}), f32[256,256]{1,0:T(8,128)}) %all-reduce.20.cloned.1.call-update) | async-done | bytes 262160 | tf_op jit(solution)/shard_map/psum | solution.py:11
  686.9 19.7 %custom-call.18 = f32[2,128,128]{1,2,0:T(8,128)S(1)} custom-call(f32[2,128,128]{2,1,0:T(8,128)S(1)} %get-tuple-element.61), custom_call_target="InvertDiagBlocksLowerTriangular" | custom-call | tf_op jit(solution)/shard_map/jit(_solve_triangular)/triangular_solve | solution.py:17
  710.3 43.4 %all-reduce.22.cloned.1.call-done = f32[3,256,256]{1,2,0:T(8,128)} async-done(((f32[3,256,256]{1,2,0:T(8,128)}), f32[3,256,256]{1,2,0:T(8,128)}) %all-reduce.22.cloned.1.call-update) | async-done | bytes 786448 | tf_op jit(solution)/shard_map/psum | solution.py:11
  756.4 59.2 %all-reduce.32.cloned.1.call-done = (f32[3,1,256,256]{2,3,0,1:T(8,128)}, f32[3,1,256,256]{2,3,0,1:T(8,128)}) async-done(((f32[3,1,256,256]{2,3,0,1:T(8,128)}, f32[3,1,256,256]{2,3,0,1:T(8,128)}), (f32[3,1,256,256]{2,3,0,1:T(8,128)}, f32[3,1,256,256]{2,3,0,1:T(8,128)})) %all-reduce.32.cloned.1.call-update) | async-done | bytes 1572880 | tf_op jit(solution)/shard_map/psum | solution.py:11
  832.1 11.7 cholesky.240
  854.2 12.0 cholesky.257
  869.9 52.9 %all-reduce.24.cloned.1.call-done = f32[256,256]{1,0:T(8,128)} async-done(((f32[256,256]{1,0:T(8,128)}), f32[256,256]{1,0:T(8,128)}) %all-reduce.24.cloned.1.call-update) | async-done | bytes 262160 | tf_op jit(solution)/shard_map/psum | solution.py:11
  927.9 19.7 %custom-call.20 = f32[2,128,128]{1,2,0:T(8,128)S(1)} custom-call(f32[2,128,128]{2,1,0:T(8,128)S(1)} %get-tuple-element.62), custom_call_target="InvertDiagBlocksLowerTriangular" | custom-call | tf_op jit(solution)/shard_map/jit(_solve_triangular)/triangular_solve | solution.py:17
  951.3 43.4 %all-reduce.26.cloned.1.call-done = f32[3,256,256]{1,2,0:T(8,128)} async-done(((f32[3,256,256]{1,2,0:T(8,128)}), f32[3,256,256]{1,2,0:T(8,128)}) %all-reduce.26.cloned.1.call-update) | async-done | bytes 786448 | tf_op jit(solution)/shard_map/psum | solution.py:11
  997.5 59.3 %all-reduce.30.cloned.1.call-done = (f32[3,1,256,256]{2,3,0,1:T(8,128)}, f32[3,1,256,256]{2,3,0,1:T(8,128)}) async-done(((f32[3,1,256,256]{2,3,0,1:T(8,128)}, f32[3,1,256,256]{2,3,0,1:T(8,128)}), (f32[3,1,256,256]{2,3,0,1:T(8,128)}, f32[3,1,256,256]{2,3,0,1:T(8,128)})) %all-reduce.30.cloned.1.call-update) | async-done | bytes 1572880 | tf_op jit(solution)/shard_map/psum | solution.py:11
  1083.8 12.1 copy.53
  1095.9 149.2 %all-reduce.28.cloned.1.call-done = f32[1,3,256,6,256]{2,4,3,1,0:T(8,128)} async-done(((f32[1,3,256,6,256]{2,4,3,1,0:T(8,128)}), f32[1,3,256,6,256]{2,4,3,1,0:T(8,128)}) %all-reduce.28.cloned.1.call-update) | async-done | bytes 4718608 | tf_op jit(solution)/shard_map/psum | solution.py:72
  (176 shorter events, 174.7 us)
Async XLA Ops:
  7.2 435.8 %all-reduce.16.cloned.1.call-start = ((), (), s32[]{:S(2)}) async-start(), calls=%async_computation | async-start | bytes 524288 | tf_op jit(solution)/shard_map/psum | solution.py:11
  31.9 104.5 %copy-start = (f32[1,3,256,1,6,256]{2,5,4,1,3,0:T(8,128)S(1)}, f32[1,3,256,1,6,256]{2,5,4,1,3,0:T(8,128)}, u32[]{:S(2)}) copy-start(f32[1,3,256,1,6,256]{2,5,4,1,3,0:T(8,128)} %copy.25) | copy-start | bytes 14155780
  34.8 101.6 %collective-permute-start = (f32[3,256,6,256]{1,3,2,0:T(8,128)S(1)}, f32[3,256,6,256]{1,3,2,0:T(8,128)S(1)}, u32[]{:S(2)}, u32[]{:S(2)}) collective-permute-start(f32[3,256,6,256]{1,3,2,0:T(8,128)S(1)} %bitcast_select_fusion.1), channel_id=1, source_target_pairs={{0,1},{1,0},{2,3},{3,2},{4,5},{5,4},{6,7},{7,6},{8,9},{9,8},{10,11... | collective-permute-start | bytes 14155784 | tf_op jit(solution)/shard_map/ppermute | solution.py:46
  139.2 203.0 %collective-permute-start.1 = (f32[3,256,6,256]{1,3,2,0:T(8,128)}, f32[3,256,6,256]{1,3,2,0:T(8,128)}, u32[]{:S(2)}, u32[]{:S(2)}) collective-permute-start(f32[3,256,6,256]{1,3,2,0:T(8,128)} %fusion.49), channel_id=1, source_target_pairs={{0,2},{1,3},{2,0},{3,1},{4,6},{5,7},{6,4},{7,5},{8,10},{9,11},{10,... | collective-permute-start | bytes 14155784 | tf_op jit(solution)/shard_map/ppermute | solution.py:46
  350.0 2.2 copy-start.2
  352.2 38.3 %slice-start = ((f32[3,256,6,256]{1,3,2,0:T(8,128)}), f32[3,256,1,256]{1,3,2,0:T(8,128)S(1)}, s32[]{:S(2)}) async-start(f32[3,256,6,256]{1,3,2,0:T(8,128)} %copy-done.2), calls=%async_computation.10 | async-start | bytes 1572864 | tf_op jit(solution)/shard_map/slice | solution.py:59
  390.0 124.9 %all-reduce.18.cloned.1.call-start = ((), (), s32[]{:S(2)}) async-start(), calls=%async_computation.1 | async-start | bytes 1572864 | tf_op jit(solution)/shard_map/psum | solution.py:11
  443.0 27.4 %copy-start.8 = (f32[256,256]{1,0:T(8,128)S(1)}, f32[256,256]{1,0:T(8,128)}, u32[]{:S(2)}) copy-start(f32[256,256]{1,0:T(8,128)} %all-reduce.16.cloned.1.call-done) | copy-start | bytes 786436
  471.6 105.5 %all-reduce.34.cloned.1.call-start = ((), (), s32[]{:S(2)}) async-start(), calls=%async_computation.9 | async-start | bytes 3145728 | tf_op jit(solution)/shard_map/psum | solution.py:11
  515.0 65.2 %copy-start.6 = (f32[3,256,256]{1,2,0:T(8,128)S(1)}, f32[3,256,256]{1,2,0:T(8,128)}, u32[]{:S(2)}) copy-start(f32[3,256,256]{1,2,0:T(8,128)} %all-reduce.18.cloned.1.call-done) | copy-start | bytes 2359300
  517.5 164.2 %all-reduce.20.cloned.1.call-start = ((), (), s32[]{:S(2)}) async-start(), calls=%async_computation.2 | async-start | bytes 524288 | tf_op jit(solution)/shard_map/psum | solution.py:11
  589.8 38.7 %slice-start.1 = ((f32[3,256,6,256]{1,3,2,0:T(8,128)}), f32[3,256,1,256]{1,3,2,0:T(8,128)S(1)}, s32[]{:S(2)}) async-start(f32[3,256,6,256]{1,3,2,0:T(8,128)} %copy-done.3), calls=%async_computation.11 | async-start | bytes 1572864 | tf_op jit(solution)/shard_map/slice | solution.py:59
  628.4 125.2 %all-reduce.22.cloned.1.call-start = ((), (), s32[]{:S(2)}) async-start(), calls=%async_computation.3 | async-start | bytes 1572864 | tf_op jit(solution)/shard_map/psum | solution.py:11
  681.7 27.3 %copy-start.10 = (f32[256,256]{1,0:T(8,128)S(1)}, f32[256,256]{1,0:T(8,128)}, u32[]{:S(2)}) copy-start(f32[256,256]{1,0:T(8,128)} %all-reduce.20.cloned.1.call-done) | copy-start | bytes 786436
  710.2 105.4 %all-reduce.32.cloned.1.call-start = ((), (), s32[]{:S(2)}) async-start(), calls=%async_computation.8 | async-start | bytes 3145728 | tf_op jit(solution)/shard_map/psum | solution.py:11
  753.6 67.7 %copy-start.5 = (f32[3,256,256]{1,2,0:T(8,128)S(1)}, f32[3,256,256]{1,2,0:T(8,128)}, u32[]{:S(2)}) copy-start(f32[3,256,256]{1,2,0:T(8,128)} %all-reduce.22.cloned.1.call-done) | copy-start | bytes 2359300
  756.1 166.7 %all-reduce.24.cloned.1.call-start = ((), (), s32[]{:S(2)}) async-start(), calls=%async_computation.4 | async-start | bytes 524288 | tf_op jit(solution)/shard_map/psum | solution.py:11
  828.6 2.2 copy-start.4
  830.9 38.8 %slice-start.2 = ((f32[3,256,6,256]{1,3,2,0:T(8,128)}), f32[3,256,1,256]{1,3,2,0:T(8,128)S(1)}, s32[]{:S(2)}) async-start(f32[3,256,6,256]{1,3,2,0:T(8,128)} %copy-done.4), calls=%async_computation.12 | async-start | bytes 1572864 | tf_op jit(solution)/shard_map/slice | solution.py:59
  869.6 125.1 %all-reduce.26.cloned.1.call-start = ((), (), s32[]{:S(2)}) async-start(), calls=%async_computation.5 | async-start | bytes 1572864 | tf_op jit(solution)/shard_map/psum | solution.py:11
  922.9 27.2 %copy-start.9 = (f32[256,256]{1,0:T(8,128)S(1)}, f32[256,256]{1,0:T(8,128)}, u32[]{:S(2)}) copy-start(f32[256,256]{1,0:T(8,128)} %all-reduce.24.cloned.1.call-done) | copy-start | bytes 786436
  951.2 105.5 %all-reduce.30.cloned.1.call-start = ((), (), s32[]{:S(2)}) async-start(), calls=%async_computation.7 | async-start | bytes 3145728 | tf_op jit(solution)/shard_map/psum | solution.py:11
  994.7 67.8 %copy-start.7 = (f32[3,256,256]{1,2,0:T(8,128)S(1)}, f32[3,256,256]{1,2,0:T(8,128)}, u32[]{:S(2)}) copy-start(f32[3,256,256]{1,2,0:T(8,128)} %all-reduce.26.cloned.1.call-done) | copy-start | bytes 2359300
  997.2 248.0 %all-reduce.28.cloned.1.call-start = ((), (), s32[]{:S(2)}) async-start(), calls=%async_computation.6 | async-start | bytes 9437184 | tf_op jit(solution)/shard_map/psum | solution.py:72
  (2 other events, 4.4 us)
Sparse Core Ops, SparseCore 0:
  390.2 52.7 all-reduce.15
  471.7 43.2 all-reduce.17
  518.9 58.2 all-reduce.33
  628.5 53.0 all-reduce.19
  710.3 43.2 all-reduce.21
  757.3 58.2 all-reduce.31
  869.7 53.0 all-reduce.23
  951.4 43.2 all-reduce.25
  998.5 58.2 all-reduce.29
  1074.0 171.1 all-reduce.27
